TPU v7x, 32 devices: a whole 2x2x4 slice. The times are simulated.
32 devices in a mesh: dp: 8 (over y, x, core), tensor: 4 (over z).
Axes of the slice: x: 2, y: 2, z: 4, core: 2. Of those that a mesh axis runs over, the one named last changes fastest.
Arguments:
- block_in: float32 [4096, 1024], P(('dp', 'tensor')), may hold values from -6 to 6
- cotangent: float32 [4096, 1024], P(('dp', 'tensor')), may hold values from -6 to 6
- routes: int32 [4096, 8], P('dp'), may hold values from 0 to 15, all different within a row; in each aligned block of 512 rows (0 to 511, 512 to 1023, ...) at most 288 rows name the same one
- gate_weights: float32 [4096, 8], P('dp'), may hold values from 0.02 to 0.3
- norm_gains: float32 [2, 1024], P(None, 'dp'), may hold values from 0.5 to 1.5
- attention_weight: float32 [4, 1024, 512], P(None, 'dp', 'tensor'), may hold values from -0.1875 to 0.1875
- output_weight: float32 [2, 1024, 512], P(None, 'dp', 'tensor'), may hold values from -0.75 to 0.75
- w_gate_up: float32 [16, 2, 1024, 512], P(None, None, 'dp', 'tensor'), may hold values from -0.1875 to 0.1875
- w_down: float32 [16, 1024, 512], P(None, 'dp', 'tensor'), may hold values from -0.75 to 0.75
- m_gains: float32 [2, 1024], P(None, 'dp'), may hold values from -128 to 128
- v_gains: float32 [2, 1024], P(None, 'dp'), may hold values from 100 to 10000
- attention_first_moment: float32 [4, 1024, 512], P(None, 'dp', 'tensor'), may hold values from -12 to 12
- attention_second_moment: float32 [4, 1024, 512], P(None, 'dp', 'tensor'), may hold values from 1 to 100
- output_first_moment: float32 [2, 1024, 512], P(None, 'dp', 'tensor'), may hold values from -16 to 16
- output_second_moment: float32 [2, 1024, 512], P(None, 'dp', 'tensor'), may hold values from 1 to 100
- m_gate_up: float32 [16, 2, 1024, 512], P(None, None, 'dp', 'tensor'), may hold values from -32 to 32
- v_gate_up: float32 [16, 2, 1024, 512], P(None, None, 'dp', 'tensor'), may hold values from 10 to 1000
- m_down: float32 [16, 1024, 512], P(None, 'dp', 'tensor'), may hold values from -12 to 12
- v_down: float32 [16, 1024, 512], P(None, 'dp', 'tensor'), may hold values from 1 to 100
Outputs:
- block_out: float32 [4096, 1024], P(('dp', 'tensor'))
- input_grad: float32 [4096, 1024], P(('dp', 'tensor'))
- grad_gains: float32 [2, 1024], P(None, 'dp')
- grad_attn: float32 [4, 1024, 512], P(None, 'dp', 'tensor')
- grad_out: float32 [2, 1024, 512], P(None, 'dp', 'tensor')
- grad_gate_up: float32 [16, 2, 1024, 512], P(None, None, 'dp', 'tensor')
- grad_down: float32 [16, 1024, 512], P(None, 'dp', 'tensor')
- new_gains: float32 [2, 1024], P(None, 'dp')
- new_attn: float32 [4, 1024, 512], P(None, 'dp', 'tensor')
- new_out: float32 [2, 1024, 512], P(None, 'dp', 'tensor')
- new_gate_up: float32 [16, 2, 1024, 512], P(None, None, 'dp', 'tensor')
- new_down: float32 [16, 1024, 512], P(None, 'dp', 'tensor')
- new_m_gains: float32 [2, 1024], P(None, 'dp')
- new_v_gains: float32 [2, 1024], P(None, 'dp')
- new_m_attn: float32 [4, 1024, 512], P(None, 'dp', 'tensor')
- new_v_attn: float32 [4, 1024, 512], P(None, 'dp', 'tensor')
- new_m_out: float32 [2, 1024, 512], P(None, 'dp', 'tensor')
- new_v_out: float32 [2, 1024, 512], P(None, 'dp', 'tensor')
- new_m_gate_up: float32 [16, 2, 1024, 512], P(None, None, 'dp', 'tensor')
- new_v_gate_up: float32 [16, 2, 1024, 512], P(None, None, 'dp', 'tensor')
- new_m_down: float32 [16, 1024, 512], P(None, 'dp', 'tensor')
- new_v_down: float32 [16, 1024, 512], P(None, 'dp', 'tensor')
Inputs may be any that keep to these rules, and one draw needn't show every extreme that they name: `routes`: each row names 8 different experts. Within each aligned block of 512 rows no expert is named by more than 288 rows, and in some block one expert is named by exactly 288 rows.
All inputs are finite; a program needn't handle non-finite values.
Results may differ from a plain program's by a relative error of at most 0.015.
The roundings to bfloat16 on the way count: a program that leaves them out, or rounds other values in their place, can miss the bound.
Values may be sent and summed in bfloat16 or wider, within the bound.
A program may use at most 192 MiB of HBM per device.

v0:
```python
import jax
import jax.numpy as jnp
from jax import lax
from jax.sharding import PartitionSpec as P

HEAD_SIZE = 64
E = 16
SEQ = 512
STEP = 3
CAP = 288


norm_eps = 1e-05
beta_one = 0.9
beta_two = 0.95
adam_eps = 1e-08
rate_matrix = 0.02
rate_gain = 0.2
decay_matrix = 0.1
rope_base = 10000.0


def rope_tables(length, width):
    half_width = width // 2
    frequency = rope_base ** (-(2.0 * jnp.arange(half_width, dtype=jnp.float32)) / width)
    angles = jnp.arange(length, dtype=jnp.float32)[:, None] * frequency[None, :]
    return (jnp.cos(angles)[:, None, :], jnp.sin(angles)[:, None, :])


def rotate(vectors, cos_table, sine_table):
    half_width = vectors.shape[-1] // 2
    lower_half = vectors[..., :half_width]
    upper_half = vectors[..., half_width:]
    return jnp.concatenate(
        [
            lower_half * cos_table - upper_half * sine_table,
            upper_half * cos_table + lower_half * sine_table,
        ],
        axis=-1,
    )


def unrotate(vectors, cos_table, sine_table):
    half_width = vectors.shape[-1] // 2
    lower_half = vectors[..., :half_width]
    upper_half = vectors[..., half_width:]
    return jnp.concatenate(
        [
            lower_half * cos_table + upper_half * sine_table,
            upper_half * cos_table - lower_half * sine_table,
        ],
        axis=-1,
    )


def causal_scores(queries, keys_rot):
    scale = queries.shape[-1] ** (-0.5)
    scores = (
        jnp.einsum("jqgh,kgh->jgqk", queries, keys_rot, preferred_element_type=jnp.float32) * scale
    )
    length = scores.shape[-1]
    allowed = lax.broadcasted_iota(jnp.int32, (length, length), 0) >= lax.broadcasted_iota(
        jnp.int32, (length, length), 1
    )
    return jnp.where(allowed, scores, -jnp.inf)


def attend(items):
    queries, keys_rot, values = items
    scores = causal_scores(queries, keys_rot)
    log_totals = jax.nn.logsumexp(scores, axis=-1)
    softmax_b = jnp.exp(scores - log_totals[..., None]).astype(jnp.bfloat16)
    attended = jnp.einsum(
        "jgqk,kgh->jqgh", softmax_b, values, preferred_element_type=jnp.float32
    ).astype(jnp.bfloat16)
    return (attended, log_totals)


def attend_back(items):
    queries, keys_rot, values, attended, log_totals, attended_cot = items
    scale = queries.shape[-1] ** (-0.5)
    scores = causal_scores(queries, keys_rot)
    softmax_f = jnp.exp(scores - log_totals[..., None])
    softmax_b = softmax_f.astype(jnp.bfloat16)
    value_cot = jnp.einsum(
        "jgqk,jqgh->kgh", softmax_b, attended_cot, preferred_element_type=jnp.float32
    )
    weight_cot = jnp.einsum(
        "jqgh,kgh->jgqk", attended_cot, values, preferred_element_type=jnp.float32
    )
    row_dots = jnp.einsum(
        "jqgh,jqgh->jgq", attended_cot, attended, preferred_element_type=jnp.float32
    )
    score_cot = (softmax_f * (weight_cot - row_dots[..., None])).astype(jnp.bfloat16)
    query_cot = (
        jnp.einsum("jgqk,kgh->jqgh", score_cot, keys_rot, preferred_element_type=jnp.float32)
        * scale
    )
    key_cot = (
        jnp.einsum("jgqk,jqgh->kgh", score_cot, queries, preferred_element_type=jnp.float32) * scale
    )
    return (query_cot, key_cot, value_cot)


def slot_table(route_rows, gate_rows, tok_count):
    hits = (route_rows[:, :, None] == jnp.arange(E, dtype=jnp.int32)[None, None, :]).astype(
        jnp.int32
    )
    per_token = jnp.sum(hits, axis=1, dtype=jnp.int32)
    before = jnp.cumsum(per_token, axis=0, dtype=jnp.int32) - per_token
    position = jnp.sum(hits * before[:, None, :], axis=2, dtype=jnp.int32)
    flat_slot = (route_rows * CAP + position).reshape(-1)
    owner = jnp.broadcast_to(
        jnp.arange(tok_count, dtype=jnp.int32)[:, None], route_rows.shape
    ).reshape(-1)
    slot_token = jnp.full((E * CAP,), tok_count, jnp.int32).at[flat_slot].set(owner)
    slot_weight = jnp.zeros((E * CAP,), jnp.float32).at[flat_slot].set(gate_rows.reshape(-1))
    return (slot_token, slot_weight)


def fetch_experts(w_gate_up, w_down, start_expert, per_turn):
    gate_up_part = w_gate_up[start_expert : start_expert + per_turn].astype(jnp.bfloat16)
    down_part = w_down[start_expert : start_expert + per_turn].astype(jnp.bfloat16)
    return (
        lax.all_gather(gate_up_part, "dp", axis=2, tiled=True),
        lax.all_gather(down_part, "dp", axis=1, tiled=True),
    )


def adamw_update(weight, moment_one, moment_two, gradient, rate, decay):
    new_one = beta_one * moment_one + (1.0 - beta_one) * gradient
    new_two = beta_two * moment_two + (1.0 - beta_two) * gradient * gradient
    corrected_one = new_one / (1.0 - beta_one**STEP)
    corrected_two = new_two / (1.0 - beta_two**STEP)
    new_weight = weight - rate * (
        corrected_one / (jnp.sqrt(corrected_two) + adam_eps) + decay * weight
    )
    return (new_weight, new_one, new_two)


def local(
    block_in,
    cotangent,
    routes,
    gate_weights,
    norm_gains,
    attention_weight,
    output_weight,
    w_gate_up,
    w_down,
    m_gains,
    v_gains,
    attention_first_moment,
    attention_second_moment,
    output_first_moment,
    output_second_moment,
    m_gate_up,
    v_gate_up,
    m_down,
    v_down,
):
    gains_all, attn_all, out_all = (
        lax.all_gather(norm_gains.astype(jnp.bfloat16), "dp", axis=1, tiled=True),
        lax.all_gather(attention_weight.astype(jnp.bfloat16), "dp", axis=1, tiled=True),
        lax.all_gather(output_weight.astype(jnp.bfloat16), "dp", axis=1, tiled=True),
    )
    tok_count = routes.shape[0]
    seq_count = tok_count // SEQ
    width = block_in.shape[1]
    kv_count = attn_all.shape[2] // HEAD_SIZE
    cos_table, sine_table = rope_tables(SEQ, HEAD_SIZE)
    gain_one = gains_all[0].astype(jnp.float32)
    gain_two = gains_all[1].astype(jnp.float32)
    inv_one = lax.rsqrt(jnp.mean(block_in * block_in, axis=1, keepdims=True) + norm_eps)
    normed_one = (block_in * inv_one * gain_one).astype(jnp.bfloat16)
    tokens_one = lax.all_gather(normed_one, "tensor", axis=0, tiled=True)
    projected = jnp.einsum("td,zdc->ztc", tokens_one, attn_all, preferred_element_type=jnp.float32)
    head_vals = projected.reshape(4, seq_count, SEQ, kv_count, HEAD_SIZE)
    queries = (
        rotate(head_vals[0:2], cos_table, sine_table).astype(jnp.bfloat16).transpose(1, 0, 2, 3, 4)
    )
    keys_rot = rotate(head_vals[2], cos_table, sine_table).astype(jnp.bfloat16)
    values = head_vals[3].astype(jnp.bfloat16)
    attended, log_totals = lax.map(attend, (queries, keys_rot, values))
    attended_flat = attended.transpose(1, 0, 2, 3, 4).reshape(2, tok_count, kv_count * HEAD_SIZE)
    partial_value = jnp.einsum(
        "jtc,jdc->td", attended_flat, out_all, preferred_element_type=jnp.float32
    )
    residual = block_in + lax.psum_scatter(partial_value, "tensor", scatter_dimension=0, tiled=True)
    inv_two = lax.rsqrt(jnp.mean(residual * residual, axis=1, keepdims=True) + norm_eps)
    normed_two = (residual * inv_two * gain_two).astype(jnp.bfloat16)
    tokens_two = lax.all_gather(normed_two, "tensor", axis=0, tiled=True)
    slot_token, slot_weight = slot_table(routes, gate_weights, tok_count)
    padded = jnp.concatenate([tokens_two, jnp.zeros((1, width), jnp.bfloat16)], axis=0)
    expert_in = padded[slot_token].reshape(E, CAP, width)
    per_turn = 8
    mixture = jnp.zeros((tok_count + 1, width), jnp.float32)
    saved_acts = []
    for start_expert in range(0, E, per_turn):
        gate_up_g, down_g = fetch_experts(w_gate_up, w_down, start_expert, per_turn)
        inputs = expert_in[start_expert : start_expert + per_turn]
        gate_up = jnp.einsum(
            "ecd,ezdf->zecf", inputs, gate_up_g, preferred_element_type=jnp.float32
        )
        hidden = (jax.nn.silu(gate_up[0]) * gate_up[1]).astype(jnp.bfloat16)
        expert_out = jnp.einsum("ecf,edf->ecd", hidden, down_g, preferred_element_type=jnp.float32)
        slot_rows = slot_token[start_expert * CAP : (start_expert + per_turn) * CAP]
        row_weight = slot_weight[start_expert * CAP : (start_expert + per_turn) * CAP]
        mixture = mixture.at[slot_rows].add(expert_out.reshape(-1, width) * row_weight[:, None])
        saved_acts.append((gate_up, hidden))
    block_out = residual + lax.psum_scatter(
        mixture[:tok_count].astype(jnp.bfloat16), "tensor", scatter_dimension=0, tiled=True
    ).astype(jnp.float32)
    cot_all = lax.all_gather(cotangent, "tensor", axis=0, tiled=True)
    cot_pad = jnp.concatenate([cot_all, jnp.zeros((1, width), jnp.float32)], axis=0)
    slot_cot = (
        (slot_weight[:, None] * cot_pad[slot_token]).astype(jnp.bfloat16).reshape(E, CAP, width)
    )
    back_sum = jnp.zeros((tok_count + 1, width), jnp.float32)
    parts_gate_up = []
    parts_down = []
    for turn_index, start_expert in enumerate(range(0, E, per_turn)):
        gate_up_g, down_g = fetch_experts(w_gate_up, w_down, start_expert, per_turn)
        gate_up, hidden = saved_acts[turn_index]
        gate_vals = gate_up[0]
        up_vals = gate_up[1]
        inputs = expert_in[start_expert : start_expert + per_turn]
        turn_cot = slot_cot[start_expert : start_expert + per_turn]
        down_local = jnp.einsum(
            "ecd,ecf->edf", turn_cot, hidden, preferred_element_type=jnp.float32
        )
        hidden_cot = jnp.einsum(
            "ecd,edf->ecf", turn_cot, down_g, preferred_element_type=jnp.float32
        )
        sigmoid_vals = jax.nn.sigmoid(gate_vals)
        gate_cot = (
            hidden_cot * up_vals * sigmoid_vals * (1.0 + gate_vals * (1.0 - sigmoid_vals))
        ).astype(jnp.bfloat16)
        up_cot = (hidden_cot * gate_vals * sigmoid_vals).astype(jnp.bfloat16)
        both_cot = jnp.stack([gate_cot, up_cot])
        gate_up_local = jnp.einsum(
            "ecd,zecf->ezdf", inputs, both_cot, preferred_element_type=jnp.float32
        )
        input_cot = jnp.einsum(
            "zecf,ezdf->ecd", both_cot, gate_up_g, preferred_element_type=jnp.float32
        )
        slot_rows = slot_token[start_expert * CAP : (start_expert + per_turn) * CAP]
        back_sum = back_sum.at[slot_rows].add(input_cot.reshape(-1, width))
        summed_gate_up, summed_down = (
            lax.psum_scatter(gate_up_local, "dp", scatter_dimension=2, tiled=True),
            lax.psum_scatter(down_local, "dp", scatter_dimension=1, tiled=True),
        )
        parts_gate_up.append(summed_gate_up)
        parts_down.append(summed_down)
    grad_gate_up = jnp.concatenate(parts_gate_up, axis=0)
    grad_down = jnp.concatenate(parts_down, axis=0)
    normed_two_cot = lax.psum_scatter(
        back_sum[:tok_count], "tensor", scatter_dimension=0, tiled=True
    )
    scaled_two = gain_two * normed_two_cot
    residual_cot = (
        cotangent
        + inv_two * scaled_two
        - residual * inv_two**3 * jnp.mean(scaled_two * residual, axis=1, keepdims=True)
    )
    resid_all = lax.all_gather(residual_cot.astype(jnp.bfloat16), "tensor", axis=0, tiled=True)
    out_local = jnp.einsum(
        "td,jtc->jdc", resid_all, attended_flat, preferred_element_type=jnp.float32
    )
    attended_cot = jnp.einsum(
        "td,jdc->jtc", resid_all, out_all, preferred_element_type=jnp.float32
    ).astype(jnp.bfloat16)
    attended_cot = attended_cot.reshape(2, seq_count, SEQ, kv_count, HEAD_SIZE).transpose(
        1, 0, 2, 3, 4
    )
    query_cot, key_cot, value_cot = lax.map(
        attend_back, (queries, keys_rot, values, attended, log_totals, attended_cot)
    )
    query_plain = (
        unrotate(query_cot, cos_table, sine_table)
        .transpose(1, 0, 2, 3, 4)
        .reshape(2, tok_count, kv_count * HEAD_SIZE)
    )
    key_plain = unrotate(key_cot, cos_table, sine_table).reshape(1, tok_count, kv_count * HEAD_SIZE)
    proj_cot = jnp.concatenate(
        [query_plain, key_plain, value_cot.reshape(1, tok_count, kv_count * HEAD_SIZE)], axis=0
    ).astype(jnp.bfloat16)
    attn_local = jnp.einsum("td,ztc->zdc", tokens_one, proj_cot, preferred_element_type=jnp.float32)
    norm_terms = jnp.einsum("ztc,zdc->td", proj_cot, attn_all, preferred_element_type=jnp.float32)
    normed_one_cot = lax.psum_scatter(
        norm_terms.astype(jnp.bfloat16), "tensor", scatter_dimension=0, tiled=True
    ).astype(jnp.float32)
    scaled_one = gain_one * normed_one_cot
    input_grad = (
        residual_cot
        + inv_one * scaled_one
        - block_in * inv_one**3 * jnp.mean(scaled_one * block_in, axis=1, keepdims=True)
    )
    gain_local = jnp.stack(
        [
            jnp.sum(normed_one_cot * block_in * inv_one, axis=0),
            jnp.sum(normed_two_cot * residual * inv_two, axis=0),
        ]
    )
    gain_part, grad_attn, grad_out = (
        lax.psum_scatter(gain_local, "dp", scatter_dimension=1, tiled=True),
        lax.psum_scatter(attn_local, "dp", scatter_dimension=1, tiled=True),
        lax.psum_scatter(out_local, "dp", scatter_dimension=1, tiled=True),
    )
    grad_gains = lax.psum(gain_part, "tensor")
    new_gains, new_m_gains, new_v_gains = adamw_update(
        norm_gains, m_gains, v_gains, grad_gains, rate_gain, 0.0
    )
    new_attn, new_m_attn, new_v_attn = adamw_update(
        attention_weight,
        attention_first_moment,
        attention_second_moment,
        grad_attn,
        rate_matrix,
        decay_matrix,
    )
    new_out, new_m_out, new_v_out = adamw_update(
        output_weight,
        output_first_moment,
        output_second_moment,
        grad_out,
        rate_matrix,
        decay_matrix,
    )
    new_gate_up, new_m_gate_up, new_v_gate_up = adamw_update(
        w_gate_up, m_gate_up, v_gate_up, grad_gate_up, rate_matrix, decay_matrix
    )
    new_down, new_m_down, new_v_down = adamw_update(
        w_down, m_down, v_down, grad_down, rate_matrix, decay_matrix
    )
    return (
        block_out,
        input_grad,
        grad_gains,
        grad_attn,
        grad_out,
        grad_gate_up,
        grad_down,
        new_gains,
        new_attn,
        new_out,
        new_gate_up,
        new_down,
        new_m_gains,
        new_v_gains,
        new_m_attn,
        new_v_attn,
        new_m_out,
        new_v_out,
        new_m_gate_up,
        new_v_gate_up,
        new_m_down,
        new_v_down,
    )


def solution(mesh):
    return jax.shard_map(
        local,
        mesh=mesh,
        in_specs=(
            P(("dp", "tensor"), None),
            P(("dp", "tensor"), None),
            P("dp", None),
            P("dp", None),
            P(None, "dp"),
            P(None, "dp", "tensor"),
            P(None, "dp", "tensor"),
            P(None, None, "dp", "tensor"),
            P(None, "dp", "tensor"),
            P(None, "dp"),
            P(None, "dp"),
            P(None, "dp", "tensor"),
            P(None, "dp", "tensor"),
            P(None, "dp", "tensor"),
            P(None, "dp", "tensor"),
            P(None, None, "dp", "tensor"),
            P(None, None, "dp", "tensor"),
            P(None, "dp", "tensor"),
            P(None, "dp", "tensor"),
        ),
        out_specs=(
            P(("dp", "tensor"), None),
            P(("dp", "tensor"), None),
            P(None, "dp"),
            P(None, "dp", "tensor"),
            P(None, "dp", "tensor"),
            P(None, None, "dp", "tensor"),
            P(None, "dp", "tensor"),
            P(None, "dp"),
            P(None, "dp", "tensor"),
            P(None, "dp", "tensor"),
            P(None, None, "dp", "tensor"),
            P(None, "dp", "tensor"),
            P(None, "dp"),
            P(None, "dp"),
            P(None, "dp", "tensor"),
            P(None, "dp", "tensor"),
            P(None, "dp", "tensor"),
            P(None, "dp", "tensor"),
            P(None, None, "dp", "tensor"),
            P(None, None, "dp", "tensor"),
            P(None, "dp", "tensor"),
            P(None, "dp", "tensor"),
        ),
        check_vma=False,
    )
```

profile of v0, /device:TPU:0, one launch (start us, length us, event | category | flops | bytes accessed | tf_op | source)
XLA Modules:
  0.0 941.4 jit_solution(5812253227274895094)
XLA Ops:
  34.1 16.2 %all-gather.10.cloned.1.call-done = bf16[512,1024]{1,0:T(8,128)(2,1)} async-done(((bf16[128,1024]{1,0:T(8,128)(2,1)}), bf16[512,1024]{1,0:T(8,128)(2,1)}) %all-gather.10.cloned.1.call-update) | async-done | bytes 1048592 | tf_op jit(solution)/shard_map/all_gather | solution.py:176
  50.3 25.3 %all-gather.12.cloned.1.call-done = bf16[4,1024,128]{1,2,0:T(8,128)(2,1)} async-done(((bf16[4,128,128]{1,2,0:T(8,128)(2,1)}), bf16[4,1024,128]{1,2,0:T(8,128)(2,1)}) %all-gather.12.cloned.1.call-update) | async-done | bytes 1048592 | tf_op jit(solution)/shard_map/all_gather | solution.py:164
  86.5 43.2 %reduce-scatter.14.cloned.1.call-done = f32[128,1024]{1,0:T(8,128)} async-done(((f32[512,1024]{1,0:T(8,128)}), f32[128,1024]{1,0:T(8,128)}) %reduce-scatter.14.cloned.1.call-update) | async-done | bytes 524304 | tf_op jit(solution)/shard_map/reduce_scatter | solution.py:189
  139.9 15.5 %scatter_custom_fusion = s32[4608]{0:T(1024)S(1)} fusion(s32[4096]{0:T(1024)S(1)} %bitcast.271, s32[4096]{0:T(1024)S(1)} %reshape.349, s32[]{:T(128)} %constant.51.clone.1), kind=kCustom, calls=%fused_computation.145 | custom fusion | bytes 18436 | tf_op jit(solution)/shard_map/scatter | solution.py:116
  155.8 15.7 %scatter_custom_fusion.1 = f32[4608]{0:T(1024)S(1)} fusion(s32[4096]{0:T(1024)S(1)} %bitcast.272, f32[4096]{0:T(1024)S(1)} %reshape.357, f32[]{:T(128)} %constant.43.clone.1), kind=kCustom, calls=%fused_computation.143 | custom fusion | bytes 18436 | tf_op jit(solution)/shard_map/scatter | solution.py:117
  177.7 15.2 %gather_fusion.1 = f32[4608,1024]{1,0:T(8,128)} fusion(f32[513,1024]{1,0:T(8,128)S(1)} %concatenate.53, s32[5120]{0:T(1024)S(1)} %pad_clamp_fusion), kind=kCustom, calls=%fused_computation.1 | custom fusion | bytes 37767168 | tf_op jit(solution)/shard_map/gather | solution.py:217
  207.0 14.9 %gather_fusion = bf16[4608,1024]{1,0:T(8,128)(2,1)} fusion(bf16[513,1024]{1,0:T(8,128)(2,1)S(1)} %concatenate.52, s32[5120]{0:T(1024)S(1)} %pad_clamp_fusion), kind=kCustom, calls=%fused_computation | custom fusion | bytes 18892800 | tf_op jit(solution)/shard_map/gather | solution.py:195
  230.6 12.5 %all-gather.16.cloned.1.call-done = bf16[8,2,1024,128]{3,2,1,0:T(8,128)(2,1)} async-done(((bf16[8,2,128,128]{3,2,1,0:T(8,128)(2,1)}), bf16[8,2,1024,128]{3,2,1,0:T(8,128)(2,1)}) %all-gather.16.cloned.1.call-update) | async-done | bytes 4194320 | tf_op jit(solution)/shard_map/all_gather | solution.py:125
  248.1 25.3 %all-gather.18.cloned.1.call-done = bf16[8,1024,128]{2,1,0:T(8,128)(2,1)} async-done(((bf16[8,128,128]{2,1,0:T(8,128)(2,1)}), bf16[8,1024,128]{2,1,0:T(8,128)(2,1)}) %all-gather.18.cloned.1.call-update) | async-done | bytes 2097168 | tf_op jit(solution)/shard_map/all_gather | solution.py:126
  283.4 24.2 %scatter_custom_fusion.4 = f32[513,1024]{1,0:T(8,128)S(1)} fusion(s32[2304]{0:T(1024)S(1)} %get-tuple-element.209, f32[2304,1024]{1,0:T(8,128)} %bitcast.236, f32[]{:T(128)} %constant.43.clone.1), kind=kCustom, calls=%fused_computation.65 | custom fusion | flops 2359296 | bytes 2101760 | tf_op jit(solution)/shard_map/scatter-add | solution.py:248
  318.9 23.9 %all-gather.22.cloned.1.call-done = bf16[8,1024,128]{2,1,0:T(8,128)(2,1)} async-done(((bf16[8,128,128]{2,1,0:T(8,128)(2,1)}), bf16[8,1024,128]{2,1,0:T(8,128)(2,1)}) %all-gather.22.cloned.1.call-update) | async-done | bytes 2097168 | tf_op jit(solution)/shard_map/all_gather | solution.py:126
  354.1 24.5 %scatter_fusion.1 = f32[513,1024]{1,0:T(8,128)S(1)} fusion(f32[513,1024]{1,0:T(8,128)S(1)} %scatter_custom_fusion.4, s32[2304]{0:T(1024)S(1)} %get-tuple-element.208, f32[2304,1024]{1,0:T(8,128)} %bitcast.233), kind=kCustom, calls=%fused_computation.7 | custom fusion | flops 2359296 | bytes 28320768 | tf_op jit(solution)/shard_map/scatter-add | solution.py:248
  387.4 24.0 %scatter_custom_fusion.2 = f32[513,1024]{1,0:T(8,128)S(1)} fusion(s32[2304]{0:T(1024)S(1)} %get-tuple-element.209, f32[2304,1024]{1,0:T(8,128)} %bitcast_multiply_fusion.1, f32[]{:T(128)} %constant.43.clone.1), kind=kCustom, calls=%fused_computation.67 | custom fusion | flops 2359296 | bytes 2101760 | tf_op jit(solution)/shard_map/scatter-add | solution.py:209
  419.0 24.1 %scatter_fusion = f32[513,1024]{1,0:T(8,128)S(1)} fusion(f32[513,1024]{1,0:T(8,128)S(1)} %scatter_custom_fusion.2, s32[2304]{0:T(1024)S(1)} %get-tuple-element.208, f32[2304,1024]{1,0:T(8,128)} %bitcast_multiply_fusion), kind=kCustom, calls=%fused_computation.5 | custom fusion | flops 2359296 | bytes 28320768 | tf_op jit(solution)/shard_map/scatter-add | solution.py:209
  445.7 26.1 %reduce-scatter.16.cloned.1.call-done = bf16[128,1024]{1,0:T(8,128)(2,1)} async-done(((bf16[512,1024]{1,0:T(8,128)(2,1)}), bf16[128,1024]{1,0:T(8,128)(2,1)}) %reduce-scatter.16.cloned.1.call-update) | async-done | bytes 262160 | tf_op jit(solution)/shard_map/reduce_scatter | solution.py:211
  474.5 26.3 %all-gather.26.cloned.1.call-done = bf16[512,1024]{1,0:T(8,128)(2,1)} async-done(((bf16[128,1024]{1,0:T(8,128)(2,1)}), bf16[512,1024]{1,0:T(8,128)(2,1)}) %all-gather.26.cloned.1.call-update) | async-done | bytes 1048592 | tf_op jit(solution)/shard_map/all_gather | solution.py:266
  572.9 18.4 %reduce-scatter.30.cloned.1.call-done = f32[8,128,128]{2,1,0:T(8,128)} async-done(((f32[8,1024,128]{2,1,0:T(8,128)}), f32[8,128,128]{2,1,0:T(8,128)}) %reduce-scatter.30.cloned.1.call-update) | async-done | bytes 524304 | tf_op jit(solution)/shard_map/reduce_scatter | solution.py:251
  592.4 53.3 %reduce-scatter.32.cloned.1.call-done = f32[8,128,128]{2,1,0:T(8,128)} async-done(((f32[8,1024,128]{2,1,0:T(8,128)}), f32[8,128,128]{2,1,0:T(8,128)}) %reduce-scatter.32.cloned.1.call-update) | async-done | bytes 524304 | tf_op jit(solution)/shard_map/reduce_scatter | solution.py:251
  650.9 34.3 %reduce-scatter.24.cloned.1.call-done = f32[2,128,128]{1,2,0:T(8,128)} async-done(((f32[2,1024,128]{1,2,0:T(8,128)}), f32[2,128,128]{1,2,0:T(8,128)}) %reduce-scatter.24.cloned.1.call-update) | async-done | bytes 131088 | tf_op jit(solution)/shard_map/reduce_scatter | solution.py:308
  692.5 29.8 %reduce-scatter.34.cloned.1.call-done = f32[128,2]{1,0:T(8,128)} async-done(((f32[1024,2]{1,0:T(8,128)}), f32[128,2]{1,0:T(8,128)}) %reduce-scatter.34.cloned.1.call-update) | async-done | bytes 1040
  723.2 11.7 %psum.7 = f32[2,128]{1,0:T(2,128)S(1)} all-reduce(f32[2,128]{1,0:T(2,128)S(1)} %copy.266), channel_id=1, replica_groups=mesh['dp'=8,'tensor'=4] {'tensor'}, use_global_device_ids=true, to_apply=%region_23.24 | all-reduce | flops 256 | bytes 2048 | tf_op jit(solution)/shard_map/psum | solution.py:310
  735.5 31.7 %reduce-scatter.22.cloned.1.call-done = f32[4,128,128]{1,2,0:T(8,128)} async-done(((f32[4,1024,128]{1,2,0:T(8,128)}), f32[4,128,128]{1,2,0:T(8,128)}) %reduce-scatter.22.cloned.1.call-update) | async-done | bytes 262160 | tf_op jit(solution)/shard_map/reduce_scatter | solution.py:307
  771.8 70.2 %reduce-scatter.26.cloned.1.call-done = f32[8,2,128,128]{2,3,1,0:T(8,128)} async-done(((f32[8,2,1024,128]{2,3,1,0:T(8,128)}), f32[8,2,128,128]{2,3,1,0:T(8,128)}) %reduce-scatter.26.cloned.1.call-update) | async-done | bytes 1048592 | tf_op jit(solution)/shard_map/reduce_scatter | solution.py:250
  843.2 73.3 %reduce-scatter.28.cloned.1.call-done = f32[8,2,128,128]{2,3,1,0:T(8,128)} async-done(((f32[8,2,1024,128]{2,3,1,0:T(8,128)}), f32[8,2,128,128]{2,3,1,0:T(8,128)}) %reduce-scatter.28.cloned.1.call-update) | async-done | bytes 1048592 | tf_op jit(solution)/shard_map/reduce_scatter | solution.py:250
  (333 shorter events, 245.8 us)
Async XLA Ops:
  7.2 43.1 %all-gather.10.cloned.1.call-start = ((), (), s32[]{:S(2)}) async-start(), calls=%async_computation.11 | async-start | bytes 1310720 | tf_op jit(solution)/shard_map/all_gather | solution.py:176
  18.2 113.1 %copy-start.63 = (f32[1,1024]{1,0:T(1,128)}, f32[1,1024]{1,0:T(1,128)S(1)}, u32[]{:S(2)}) copy-start(f32[1,1024]{1,0:T(1,128)S(1)} %get-tuple-element.210) | copy-start | bytes 12292
  21.8 53.8 %all-gather.12.cloned.1.call-start = ((), (), s32[]{:S(2)}) async-start(), calls=%async_computation.12 | async-start | bytes 1179648 | tf_op jit(solution)/shard_map/all_gather | solution.py:164
  23.7 105.9 %reduce-scatter.14.cloned.1.call-start = ((), (), s32[]{:S(2)}) async-start(), calls=%async_computation.13 | async-start | bytes 2621440 | tf_op jit(solution)/shard_map/reduce_scatter | solution.py:189
  85.8 90.1 %all-gather.24.cloned.1.call-start = ((), (), s32[]{:S(2)}) async-start(), calls=%async_computation.20 | async-start | bytes 2621440 | tf_op jit(solution)/shard_map/all_gather | solution.py:214
  86.4 119.2 %all-gather.14.cloned.1.call-start = ((), (), s32[]{:S(2)}) async-start(), calls=%async_computation.14 | async-start | bytes 1310720 | tf_op jit(solution)/shard_map/all_gather | solution.py:192
  132.7 110.4 %all-gather.16.cloned.1.call-start = ((), (), s32[]{:S(2)}) async-start(), calls=%async_computation.15 | async-start | bytes 4718592 | tf_op jit(solution)/shard_map/all_gather | solution.py:125
  134.0 139.4 %all-gather.18.cloned.1.call-start = ((), (), s32[]{:S(2)}) async-start(), calls=%async_computation.16 | async-start | bytes 2359296 | tf_op jit(solution)/shard_map/all_gather | solution.py:126
  136.2 176.2 %all-gather.20.cloned.1.call-start = ((), (), s32[]{:S(2)}) async-start(), calls=%async_computation.17 | async-start | bytes 4718592 | tf_op jit(solution)/shard_map/all_gather | solution.py:125
  137.0 205.8 %all-gather.22.cloned.1.call-start = ((), (), s32[]{:S(2)}) async-start(), calls=%async_computation.18 | async-start | bytes 2359296 | tf_op jit(solution)/shard_map/all_gather | solution.py:126
  137.7 306.6 %reduce-scatter.18.cloned.1.call-start = ((), (), s32[]{:S(2)}) async-start(), calls=%async_computation.21 | async-start | bytes 2621440 | tf_op jit(solution)/shard_map/reduce_scatter | solution.py:257
  380.1 91.7 %reduce-scatter.16.cloned.1.call-start = ((), (), s32[]{:S(2)}) async-start(), calls=%async_computation.19 | async-start | bytes 1310720 | tf_op jit(solution)/shard_map/reduce_scatter | solution.py:211
  444.3 56.5 %all-gather.26.cloned.1.call-start = ((), (), s32[]{:S(2)}) async-start(), calls=%async_computation.22 | async-start | bytes 1310720 | tf_op jit(solution)/shard_map/all_gather | solution.py:266
  474.2 64.3 %reduce-scatter.20.cloned.1.call-start = ((), (), s32[]{:S(2)}) async-start(), calls=%async_computation.23 | async-start | bytes 1310720 | tf_op jit(solution)/shard_map/reduce_scatter | solution.py:290
  511.6 79.7 %reduce-scatter.30.cloned.1.call-start = ((), (), s32[]{:S(2)}) async-start(), calls=%async_computation.28 | async-start | bytes 4718592 | tf_op jit(solution)/shard_map/reduce_scatter | solution.py:251
  518.2 127.5 %reduce-scatter.32.cloned.1.call-start = ((), (), s32[]{:S(2)}) async-start(), calls=%async_computation.29 | async-start | bytes 4718592 | tf_op jit(solution)/shard_map/reduce_scatter | solution.py:251
  525.7 159.5 %reduce-scatter.24.cloned.1.call-start = ((), (), s32[]{:S(2)}) async-start(), calls=%async_computation.25 | async-start | bytes 1179648 | tf_op jit(solution)/shard_map/reduce_scatter | solution.py:308
  528.3 194.0 %reduce-scatter.34.cloned.1.call-start = ((), (), s32[]{:S(2)}) async-start(), calls=%async_computation.30 | async-start | bytes 589824
  541.2 226.0 %reduce-scatter.22.cloned.1.call-start = ((), (), s32[]{:S(2)}) async-start(), calls=%async_computation.24 | async-start | bytes 2359296 | tf_op jit(solution)/shard_map/reduce_scatter | solution.py:307
  543.3 298.6 %reduce-scatter.26.cloned.1.call-start = ((), (), s32[]{:S(2)}) async-start(), calls=%async_computation.26 | async-start | bytes 9437184 | tf_op jit(solution)/shard_map/reduce_scatter | solution.py:250
  552.0 364.5 %reduce-scatter.28.cloned.1.call-start = ((), (), s32[]{:S(2)}) async-start(), calls=%async_computation.27 | async-start | bytes 9437184 | tf_op jit(solution)/shard_map/reduce_scatter | solution.py:250
  650.9 84.0 %copy-start.73 = (f32[2,128]{1,0:T(2,128)S(1)}, f32[2,128]{1,0:T(2,128)}, u32[]{:S(2)}) copy-start(f32[2,128]{1,0:T(2,128)} %param.23) | copy-start | bytes 3076
  650.9 116.3 %copy-start.24 = (f32[4,128,128]{1,2,0:T(8,128)S(1)}, f32[4,128,128]{1,2,0:T(8,128)}, u32[]{:S(2)}) copy-start(f32[4,128,128]{1,2,0:T(8,128)} %copy-done.23) | copy-start | bytes 786436
  734.9 108.4 %copy-start.72 = (f32[2,128]{1,0:T(2,128)}, f32[2,128]{1,0:T(2,128)S(1)}, u32[]{:S(2)}) copy-start(f32[2,128]{1,0:T(2,128)S(1)} %psum.7) | copy-start | bytes 3076
  (73 other events, 880.3 us)
Sparse Core Ops, SparseCore 0:
  21.9 28.2 all-gather.9
  52.7 22.8 all-gather.11
  85.9 43.6 reduce-scatter.13
  131.0 44.8 all-gather.23
  177.9 26.7 all-gather.13
  207.1 35.9 all-gather.15
  245.6 27.7 all-gather.17
  275.9 36.5 all-gather.19
  315.0 27.7 all-gather.21
  380.2 43.6 reduce-scatter.17
  444.4 27.3 reduce-scatter.15
  474.3 26.4 all-gather.25
  511.7 26.6 reduce-scatter.19
  541.7 49.5 reduce-scatter.29
  594.5 51.0 reduce-scatter.31
  649.2 35.9 reduce-scatter.23
  688.1 34.1 reduce-scatter.33
  726.0 41.1 reduce-scatter.21
  770.6 71.2 reduce-scatter.25
  845.2 71.2 reduce-scatter.27
where the time goes:
time: 950 us; the launch traced here: 941 us
  waiting for transfers between devices  531 us (56%)
  other arithmetic  148 us (16%)
  local copies, waits for them, and re-layouts  130 us (14%)
  matrix products  83.6 us (9%)
  blocking collectives  31.8 us (3%)
  between operations  15.9 us (2%)
    reduce_scatter x2, waiting for transfers between devices, local(): lax.psum_scatter(gate_up_local, 'dp', scatter_dimension=2, tiled=True)  143 us
    reduce_scatter x2, waiting for transfers between devices, local(): lax.psum_scatter(down_local, 'dp', scatter_dimension=1, tiled=True)  71.7 us
    all_gather x2, waiting for transfers between devices, fetch_experts(): lax.all_gather(down_part, 'dp', axis=1, tiled=True)  49.2 us
    scatter-add x2, other arithmetic, local(): back_sum = back_sum.at[slot_rows].add(input_cot.reshape(-1, width))  48.7 us
    scatter-add x2, other arithmetic, local(): mixture.at[slot_rows]  48.1 us
    unnamed x180, local copies, waits for them, and re-layouts  43.3 us
    reduce_scatter x1, waiting for transfers between devices, local(): lax.psum_scatter(partial_value, 'tensor', scatter_dimension=0, tiled=True)  43.2 us
    reduce_scatter x1, waiting for transfers between devices, local(): lax.psum_scatter(out_local, 'dp', scatter_dimension=1, tiled=True)  34.3 us
  transfers between devices with their start and end apart: 20, of which 18 were waited for; matrix products, arithmetic and copies ran while one was open for 29% of the time, Pallas kernels for 0%

commit v1 on v0

v1 whole, which is shorter than its diff:
```python
import jax
import jax.numpy as jnp
from jax import lax
from jax.sharding import PartitionSpec as P

HEAD_SIZE = 64
SEQ = 512
STEP = 3


norm_eps = 1e-05
beta_one = 0.9
beta_two = 0.95
adam_eps = 1e-08
rate_matrix = 0.02
rate_gain = 0.2
decay_matrix = 0.1
rope_base = 10000.0


def rope_tables(length, width):
    half_width = width // 2
    frequency = rope_base ** (-(2.0 * jnp.arange(half_width, dtype=jnp.float32)) / width)
    angles = jnp.arange(length, dtype=jnp.float32)[:, None] * frequency[None, :]
    return (jnp.cos(angles)[:, None, :], jnp.sin(angles)[:, None, :])


def rotate(vectors, cos_table, sine_table):
    half_width = vectors.shape[-1] // 2
    lower_half = vectors[..., :half_width]
    upper_half = vectors[..., half_width:]
    return jnp.concatenate(
        [
            lower_half * cos_table - upper_half * sine_table,
            upper_half * cos_table + lower_half * sine_table,
        ],
        axis=-1,
    )


def unrotate(vectors, cos_table, sine_table):
    half_width = vectors.shape[-1] // 2
    lower_half = vectors[..., :half_width]
    upper_half = vectors[..., half_width:]
    return jnp.concatenate(
        [
            lower_half * cos_table + upper_half * sine_table,
            upper_half * cos_table - lower_half * sine_table,
        ],
        axis=-1,
    )


def causal_scores(queries, keys_rot):
    scale = queries.shape[-1] ** (-0.5)
    scores = (
        jnp.einsum("jqgh,kgh->jgqk", queries, keys_rot, preferred_element_type=jnp.float32) * scale
    )
    length = scores.shape[-1]
    allowed = lax.broadcasted_iota(jnp.int32, (length, length), 0) >= lax.broadcasted_iota(
        jnp.int32, (length, length), 1
    )
    return jnp.where(allowed, scores, -jnp.inf)


def attend(items):
    queries, keys_rot, values = items
    scores = causal_scores(queries, keys_rot)
    log_totals = jax.nn.logsumexp(scores, axis=-1)
    softmax_b = jnp.exp(scores - log_totals[..., None]).astype(jnp.bfloat16)
    attended = jnp.einsum(
        "jgqk,kgh->jqgh", softmax_b, values, preferred_element_type=jnp.float32
    ).astype(jnp.bfloat16)
    return (attended, log_totals)


def attend_back(items):
    queries, keys_rot, values, attended, log_totals, attended_cot = items
    scale = queries.shape[-1] ** (-0.5)
    scores = causal_scores(queries, keys_rot)
    softmax_f = jnp.exp(scores - log_totals[..., None])
    softmax_b = softmax_f.astype(jnp.bfloat16)
    value_cot = jnp.einsum(
        "jgqk,jqgh->kgh", softmax_b, attended_cot, preferred_element_type=jnp.float32
    )
    weight_cot = jnp.einsum(
        "jqgh,kgh->jgqk", attended_cot, values, preferred_element_type=jnp.float32
    )
    row_dots = jnp.einsum(
        "jqgh,jqgh->jgq", attended_cot, attended, preferred_element_type=jnp.float32
    )
    score_cot = (softmax_f * (weight_cot - row_dots[..., None])).astype(jnp.bfloat16)
    query_cot = (
        jnp.einsum("jgqk,kgh->jqgh", score_cot, keys_rot, preferred_element_type=jnp.float32)
        * scale
    )
    key_cot = (
        jnp.einsum("jgqk,jqgh->kgh", score_cot, queries, preferred_element_type=jnp.float32) * scale
    )
    return (query_cot, key_cot, value_cot)


def adamw_update(weight, moment_one, moment_two, gradient, rate, decay):
    new_one = beta_one * moment_one + (1.0 - beta_one) * gradient
    new_two = beta_two * moment_two + (1.0 - beta_two) * gradient * gradient
    corrected_one = new_one / (1.0 - beta_one**STEP)
    corrected_two = new_two / (1.0 - beta_two**STEP)
    new_weight = weight - rate * (
        corrected_one / (jnp.sqrt(corrected_two) + adam_eps) + decay * weight
    )
    return (new_weight, new_one, new_two)


def local(
    block_in,
    cotangent,
    routes,
    gate_weights,
    norm_gains,
    attention_weight,
    output_weight,
    w_gate_up,
    w_down,
    m_gains,
    v_gains,
    attention_first_moment,
    attention_second_moment,
    output_first_moment,
    output_second_moment,
    m_gate_up,
    v_gate_up,
    m_down,
    v_down,
):
    bf = jnp.bfloat16
    f32 = jnp.float32
    tok_count = routes.shape[0]
    seq_count = tok_count // SEQ
    width = block_in.shape[1]
    experts = w_gate_up.shape[0]
    rows = w_gate_up.shape[2]
    units = w_gate_up.shape[3]
    cols = attention_weight.shape[2]
    kv_count = cols // HEAD_SIZE
    gains_all = lax.all_gather(norm_gains.astype(bf), "dp", axis=1, tiled=True)
    attn_rows = jnp.concatenate([attention_weight, output_weight], axis=0)
    attn_rows = attn_rows.astype(bf).transpose(1, 0, 2).reshape(rows, 6 * cols)
    attn_all = lax.all_gather(attn_rows, "dp", axis=0, tiled=True)
    proj_all = attn_all[:, : 4 * cols]
    out_all = attn_all[:, 4 * cols :]
    gate_up_rows = w_gate_up.astype(bf).transpose(2, 1, 0, 3).reshape(rows, 2 * experts * units)
    down_rows = w_down.astype(bf).transpose(1, 0, 2).reshape(rows, experts * units)

    cos_table, sine_table = rope_tables(SEQ, HEAD_SIZE)
    gain_one = gains_all[0].astype(f32)
    gain_two = gains_all[1].astype(f32)
    inv_one = lax.rsqrt(jnp.mean(block_in * block_in, axis=1, keepdims=True) + norm_eps)
    normed_one = (block_in * inv_one * gain_one).astype(bf)
    tokens_one = lax.all_gather(normed_one, "tensor", axis=0, tiled=True)
    gate_up_all = lax.all_gather(gate_up_rows, "dp", axis=0, tiled=True)
    down_all = lax.all_gather(down_rows, "dp", axis=0, tiled=True)
    cot_all = lax.all_gather(cotangent.astype(bf), "tensor", axis=0, tiled=True)
    projected = jnp.dot(tokens_one, proj_all, preferred_element_type=f32)
    head_vals = projected.reshape(seq_count, SEQ, 4, kv_count, HEAD_SIZE).transpose(2, 0, 1, 3, 4)
    queries = (
        rotate(head_vals[0:2], cos_table, sine_table).astype(bf).transpose(1, 0, 2, 3, 4)
    )
    keys_rot = rotate(head_vals[2], cos_table, sine_table).astype(bf)
    values = head_vals[3].astype(bf)
    attended, log_totals = lax.map(attend, (queries, keys_rot, values))
    attended_flat = attended.transpose(0, 2, 1, 3, 4).reshape(tok_count, 2 * cols)
    partial_value = jnp.dot(attended_flat, out_all.T, preferred_element_type=f32).astype(bf)
    residual = block_in + lax.psum_scatter(
        partial_value, "tensor", scatter_dimension=0, tiled=True
    ).astype(f32)
    inv_two = lax.rsqrt(jnp.mean(residual * residual, axis=1, keepdims=True) + norm_eps)
    normed_two = (residual * inv_two * gain_two).astype(bf)
    tokens_two = lax.all_gather(normed_two, "tensor", axis=0, tiled=True)
    expert_ids = jnp.arange(experts, dtype=jnp.int32)[None, None, :]
    token_weight = jnp.sum(
        jnp.where(routes[:, :, None] == expert_ids, gate_weights[:, :, None], 0.0), axis=1
    )
    weight_wide = jnp.broadcast_to(
        token_weight[:, :, None], (tok_count, experts, units)
    ).reshape(tok_count, experts * units)
    half = experts * units
    gate_up = jnp.dot(tokens_two, gate_up_all, preferred_element_type=f32)
    gate_vals = gate_up[:, :half]
    up_vals = gate_up[:, half:]
    sigmoid_vals = jax.nn.sigmoid(gate_vals)
    hidden = (gate_vals * sigmoid_vals * up_vals * weight_wide).astype(bf)
    hidden_cot = jnp.dot(cot_all, down_all, preferred_element_type=f32) * weight_wide
    gate_cot = (
        hidden_cot * up_vals * sigmoid_vals * (1.0 + gate_vals * (1.0 - sigmoid_vals))
    ).astype(bf)
    up_cot = (hidden_cot * gate_vals * sigmoid_vals).astype(bf)
    both_cot = jnp.concatenate([gate_cot, up_cot], axis=1)
    back_sum = lax.dot_general(
        both_cot, gate_up_all, (((1,), (1,)), ((), ())), preferred_element_type=f32
    ).astype(bf)
    normed_two_cot = lax.psum_scatter(
        back_sum, "tensor", scatter_dimension=0, tiled=True
    ).astype(f32)
    down_local = lax.dot_general(
        cot_all, hidden, (((0,), (0,)), ((), ())), preferred_element_type=f32
    ).astype(bf)
    gate_up_local = lax.dot_general(
        tokens_two, both_cot, (((0,), (0,)), ((), ())), preferred_element_type=f32
    ).astype(bf)
    mixture = lax.dot_general(
        hidden, down_all, (((1,), (1,)), ((), ())), preferred_element_type=f32
    ).astype(bf)
    block_out = residual + lax.psum_scatter(
        mixture, "tensor", scatter_dimension=0, tiled=True
    ).astype(f32)
    grad_down = lax.psum_scatter(down_local, "dp", scatter_dimension=0, tiled=True)
    grad_down = grad_down.astype(f32).reshape(rows, experts, units).transpose(1, 0, 2)
    grad_gate_up = lax.psum_scatter(gate_up_local, "dp", scatter_dimension=0, tiled=True)
    grad_gate_up = (
        grad_gate_up.astype(f32).reshape(rows, 2, experts, units).transpose(2, 1, 0, 3)
    )
    scaled_two = gain_two * normed_two_cot
    residual_cot = (
        cotangent
        + inv_two * scaled_two
        - residual * inv_two**3 * jnp.mean(scaled_two * residual, axis=1, keepdims=True)
    )
    resid_all = lax.all_gather(residual_cot.astype(bf), "tensor", axis=0, tiled=True)
    out_local = lax.dot_general(
        resid_all, attended_flat, (((0,), (0,)), ((), ())), preferred_element_type=f32
    )
    attended_cot = jnp.dot(resid_all, out_all, preferred_element_type=f32).astype(bf)
    attended_cot = attended_cot.reshape(seq_count, SEQ, 2, kv_count, HEAD_SIZE).transpose(
        0, 2, 1, 3, 4
    )
    query_cot, key_cot, value_cot = lax.map(
        attend_back, (queries, keys_rot, values, attended, log_totals, attended_cot)
    )
    query_plain = unrotate(query_cot, cos_table, sine_table)
    key_plain = unrotate(key_cot, cos_table, sine_table)
    proj_cot = jnp.concatenate(
        [
            query_plain[:, 0].reshape(tok_count, cols),
            query_plain[:, 1].reshape(tok_count, cols),
            key_plain.reshape(tok_count, cols),
            value_cot.reshape(tok_count, cols),
        ],
        axis=1,
    ).astype(bf)
    attn_local = lax.dot_general(
        tokens_one, proj_cot, (((0,), (0,)), ((), ())), preferred_element_type=f32
    )
    norm_terms = lax.dot_general(
        proj_cot, proj_all, (((1,), (1,)), ((), ())), preferred_element_type=f32
    )
    normed_one_cot = lax.psum_scatter(
        norm_terms.astype(bf), "tensor", scatter_dimension=0, tiled=True
    ).astype(f32)
    both_local = jnp.concatenate([attn_local, out_local], axis=1).astype(bf)
    both_sum = lax.psum_scatter(both_local, "dp", scatter_dimension=0, tiled=True).astype(f32)
    both_sum = both_sum.reshape(rows, 6, cols).transpose(1, 0, 2)
    grad_attn = both_sum[:4]
    grad_out = both_sum[4:]
    scaled_one = gain_one * normed_one_cot
    input_grad = (
        residual_cot
        + inv_one * scaled_one
        - block_in * inv_one**3 * jnp.mean(scaled_one * block_in, axis=1, keepdims=True)
    )
    gain_local = jnp.stack(
        [
            jnp.sum(normed_one_cot * block_in * inv_one, axis=0),
            jnp.sum(normed_two_cot * residual * inv_two, axis=0),
        ]
    )
    gain_sum = lax.psum(gain_local, ("dp", "tensor"))
    grad_gains = lax.dynamic_slice_in_dim(gain_sum, lax.axis_index("dp") * rows, rows, axis=1)
    new_gains, new_m_gains, new_v_gains = adamw_update(
        norm_gains, m_gains, v_gains, grad_gains, rate_gain, 0.0
    )
    new_attn, new_m_attn, new_v_attn = adamw_update(
        attention_weight,
        attention_first_moment,
        attention_second_moment,
        grad_attn,
        rate_matrix,
        decay_matrix,
    )
    new_out, new_m_out, new_v_out = adamw_update(
        output_weight,
        output_first_moment,
        output_second_moment,
        grad_out,
        rate_matrix,
        decay_matrix,
    )
    new_gate_up, new_m_gate_up, new_v_gate_up = adamw_update(
        w_gate_up, m_gate_up, v_gate_up, grad_gate_up, rate_matrix, decay_matrix
    )
    new_down, new_m_down, new_v_down = adamw_update(
        w_down, m_down, v_down, grad_down, rate_matrix, decay_matrix
    )
    return (
        block_out,
        input_grad,
        grad_gains,
        grad_attn,
        grad_out,
        grad_gate_up,
        grad_down,
        new_gains,
        new_attn,
        new_out,
        new_gate_up,
        new_down,
        new_m_gains,
        new_v_gains,
        new_m_attn,
        new_v_attn,
        new_m_out,
        new_v_out,
        new_m_gate_up,
        new_v_gate_up,
        new_m_down,
        new_v_down,
    )


def solution(mesh):
    return jax.shard_map(
        local,
        mesh=mesh,
        in_specs=(
            P(("dp", "tensor"), None),
            P(("dp", "tensor"), None),
            P("dp", None),
            P("dp", None),
            P(None, "dp"),
            P(None, "dp", "tensor"),
            P(None, "dp", "tensor"),
            P(None, None, "dp", "tensor"),
            P(None, "dp", "tensor"),
            P(None, "dp"),
            P(None, "dp"),
            P(None, "dp", "tensor"),
            P(None, "dp", "tensor"),
            P(None, "dp", "tensor"),
            P(None, "dp", "tensor"),
            P(None, None, "dp", "tensor"),
            P(None, None, "dp", "tensor"),
            P(None, "dp", "tensor"),
            P(None, "dp", "tensor"),
        ),
        out_specs=(
            P(("dp", "tensor"), None),
            P(("dp", "tensor"), None),
            P(None, "dp"),
            P(None, "dp", "tensor"),
            P(None, "dp", "tensor"),
            P(None, None, "dp", "tensor"),
            P(None, "dp", "tensor"),
            P(None, "dp"),
            P(None, "dp", "tensor"),
            P(None, "dp", "tensor"),
            P(None, None, "dp", "tensor"),
            P(None, "dp", "tensor"),
            P(None, "dp"),
            P(None, "dp"),
            P(None, "dp", "tensor"),
            P(None, "dp", "tensor"),
            P(None, "dp", "tensor"),
            P(None, "dp", "tensor"),
            P(None, None, "dp", "tensor"),
            P(None, None, "dp", "tensor"),
            P(None, "dp", "tensor"),
            P(None, "dp", "tensor"),
        ),
        check_vma=False,
    )
```

time: 950 us -> 605 us (0.64)
  waiting for transfers between devices: 531 us -> 403 us
  other arithmetic: 148 us -> 34.6 us
  local copies, waits for them, and re-layouts: 130 us -> 29 us
  blocking collectives: 31.8 us -> 50.3 us
  matrix products: 83.6 us -> 66.3 us
    reduce_scatter x9 -> x4, waiting for transfers between devices: 317 us -> 116 us  [the longest x1 68.6 us: local(): lax.psum_scatter(gate_up_local, 'dp', scatter_dimension=0, tiled=True)]
    scatter-add x4 -> x0, other arithmetic: 96.8 us -> none  [the longest x2 48.7 us: local(): back_sum = back_sum.at[slot_rows].add(input_cot.reshape(-1, width))]
    all_gather x7 -> x5, waiting for transfers between devices: 123 us -> 169 us  [the longest x1 57.6 us: local(): gate_up_all = lax.all_gather(gate_up_rows, 'dp', axis=0, tiled=True)]
    scatter x2 -> x0, local copies, waits for them, and re-layouts: 31.3 us -> none  [the longest x1 15.7 us: slot_table(): jnp.zeros((E * CAP,), jnp.float32).at[flat_slot].set(gate_rows.reshape(-1))]
    gather x2 -> x0, local copies, waits for them, and re-layouts: 30.2 us -> none  [the longest x1 15.2 us: local(): cot_pad[slot_token]]
    psum x1, blocking collectives: 11.7 us -> 40 us  [local(): gain_sum = lax.psum(gain_local, ('dp', 'tensor'))]
    unnamed x180 -> x95, local copies, waits for them, and re-layouts: 43.3 us -> 24.6 us
    slice x12 -> x1, local copies, waits for them, and re-layouts: 18.2 us -> 0.02 us  [local(): query_plain[:, 0].reshape(tok_count, cols)]
  transfers between devices with their start and end apart: 20 -> 14, of which waited for: 18 -> 12; matrix products, arithmetic and copies ran while one was open for 29% -> 12% of each run, Pallas kernels for 0% -> 0%
where the time goes in v1:
time: 605 us; the launch traced here: 599 us
  waiting for transfers between devices  403 us (67%)
  matrix products  66.3 us (11%)
  blocking collectives  50.3 us (8%)
  other arithmetic  34.6 us (6%)
  local copies, waits for them, and re-layouts  29 us (5%)
  between operations  15.1 us (2%)
    reduce_scatter x1, waiting for transfers between devices, local(): lax.psum_scatter(gate_up_local, 'dp', scatter_dimension=0, tiled=True)  68.6 us
    all_gather x1, waiting for transfers between devices, local(): gate_up_all = lax.all_gather(gate_up_rows, 'dp', axis=0, tiled=True)  57.6 us
    unnamed x16, waiting for transfers between devices  48 us
    psum x1, blocking collectives, local(): gain_sum = lax.psum(gain_local, ('dp', 'tensor'))  40 us
    all_gather x1, waiting for transfers between devices, local(): down_all = lax.all_gather(down_rows, 'dp', axis=0, tiled=True)  39.2 us
    all_gather x1, waiting for transfers between devices, local(): attn_all = lax.all_gather(attn_rows, 'dp', axis=0, tiled=True)  27.6 us
    reduce_scatter x1, waiting for transfers between devices, local(): lax.psum_scatter(partial_value, 'tensor', scatter_dimension=0, tiled=True)  27.4 us
    all_gather x1, waiting for transfers between devices, local(): lax.all_gather(residual_cot.astype(bf), 'tensor', axis=0, tiled=True)  26.6 us
  transfers between devices with their start and end apart: 14, of which 12 were waited for; matrix products, arithmetic and copies ran while one was open for 12% of the time, Pallas kernels for 0%

profile of v1, /device:TPU:0, one launch (start us, length us, event | category | flops | bytes accessed | tf_op | source)
XLA Modules:
  0.0 599.0 jit_solution(3122732607899009950)
XLA Ops:
  7.9 10.3 %all_gather.24 = bf16[2,1024]{1,0:T(2,128)(2,1)S(1)} all-gather(bf16[2,128]{1,0:T(2,128)(2,1)S(1)} %convert_element_type.108), channel_id=1, replica_groups=mesh['dp'=8,'tensor'=4] {'dp'}, dimensions={1}, use_global_device_ids=true | all-gather | bytes 4608 | tf_op jit(solution)/shard_map/all_gather | solution.py:145
  25.1 25.1 %all-gather.8.cloned.1.call-done = bf16[512,1024]{1,0:T(8,128)(2,1)} async-done(((bf16[128,1024]{1,0:T(8,128)(2,1)}), bf16[512,1024]{1,0:T(8,128)(2,1)}) %all-gather.8.cloned.1.call-update) | async-done | bytes 1048592 | tf_op jit(solution)/shard_map/all_gather | solution.py:159
  50.2 27.6 %all-gather.10.cloned.1.call-done = bf16[1024,768]{0,1:T(8,128)(2,1)} async-done(((bf16[128,768]{0,1:T(8,128)(2,1)}), bf16[1024,768]{0,1:T(8,128)(2,1)}) %all-gather.10.cloned.1.call-update) | async-done | bytes 1572880 | tf_op jit(solution)/shard_map/all_gather | solution.py:148
  87.2 27.4 %reduce-scatter.12.cloned.1.call-done = bf16[128,1024]{1,0:T(8,128)(2,1)} async-done(((bf16[512,1024]{1,0:T(8,128)(2,1)}), bf16[128,1024]{1,0:T(8,128)(2,1)}) %reduce-scatter.12.cloned.1.call-update) | async-done | bytes 262160 | tf_op jit(solution)/shard_map/reduce_scatter | solution.py:173
  127.6 16.6 %all-gather.12.cloned.1.call-done = bf16[512,1024]{1,0:T(8,128)(2,1)} async-done(((bf16[128,1024]{1,0:T(8,128)(2,1)}), bf16[512,1024]{1,0:T(8,128)(2,1)}) %all-gather.12.cloned.1.call-update) | async-done | bytes 1048592 | tf_op jit(solution)/shard_map/all_gather | solution.py:178
  144.2 57.6 %all-gather.14.cloned.1.call-done = bf16[1024,4096]{0,1:T(8,128)(2,1)} async-done(((bf16[128,4096]{0,1:T(8,128)(2,1)}), bf16[1024,4096]{0,1:T(8,128)(2,1)}) %all-gather.14.cloned.1.call-update) | async-done | bytes 8388624 | tf_op jit(solution)/shard_map/all_gather | solution.py:160
  201.8 11.5 %fusion.68 = f32[512,4096]{1,0:T(8,128)} fusion(bf16[512,1024]{1,0:T(8,128)(2,1)} %all-gather.12.cloned.1.call-done, bf16[1024,4096]{0,1:T(8,128)(2,1)} %all-gather.14.cloned.1.call-done), kind=kOutput, calls=%fused_computation.141 | convolution fusion | flops 4294967296 | bytes 17825792 | tf_op jit(solution)/shard_map/dot_general | solution.py:187
  213.3 18.5 %all-gather.18.cloned.1.call-done = bf16[512,1024]{1,0:T(8,128)(2,1)} async-done(((bf16[128,1024]{1,0:T(8,128)(2,1)}), bf16[512,1024]{1,0:T(8,128)(2,1)}) %all-gather.18.cloned.1.call-update) | async-done | bytes 1048592 | tf_op jit(solution)/shard_map/all_gather | solution.py:162
  231.8 39.2 %all-gather.16.cloned.1.call-done = bf16[1024,2048]{0,1:T(8,128)(2,1)} async-done(((bf16[128,2048]{0,1:T(8,128)(2,1)}), bf16[1024,2048]{0,1:T(8,128)(2,1)}) %all-gather.16.cloned.1.call-update) | async-done | bytes 4194320 | tf_op jit(solution)/shard_map/all_gather | solution.py:161
  273.2 10.1 %multiply_convert_fusion.1 = (bf16[512,2048]{1,0:T(8,128)(2,1)S(1)}, bf16[512,2048]{1,0:T(8,128)(2,1)S(1)}, bf16[512,2048]{1,0:T(8,128)(2,1)}) fusion(f32[512,4096]{1,0:T(8,128)} %fusion.68, f32[64,8,16,128]{3,2,1,0:T(8,128)S(1)} %bitcast.152, bf16[512,1024]{1,0:T(8,128)(2,1)} %all-gather.18.cloned.1.call-done, ...), kind=kOutput, calls=%fused_computation.11 | convolution fusion | flops 2166358016 | bytes 24117248 | tf_op jit(solution)/shard_map/dot_general | solution.py:192
  285.4 5.5 fusion.9
  291.1 6.1 %convolution_convert_fusion.4 = bf16[512,1024]{1,0:T(8,128)(2,1)} fusion(bf16[512,2048]{1,0:T(8,128)(2,1)} %get-tuple-element.99, bf16[1024,2048]{0,1:T(8,128)(2,1)} %all-gather.16.cloned.1.call-done), kind=kOutput, calls=%fused_computation.32 | convolution fusion | flops 2148007936 | bytes 7340032 | tf_op jit(solution)/shard_map/dot_general | solution.py:210
  297.3 21.0 %reduce-scatter.16.cloned.1.call-done = bf16[128,1024]{1,0:T(8,128)(2,1)} async-done(((bf16[512,1024]{1,0:T(8,128)(2,1)}), bf16[128,1024]{1,0:T(8,128)(2,1)}) %reduce-scatter.16.cloned.1.call-update) | async-done | bytes 262160 | tf_op jit(solution)/shard_map/reduce_scatter | solution.py:201
  320.5 26.5 %reduce-scatter.14.cloned.1.call-done = bf16[128,1024]{1,0:T(8,128)(2,1)} async-done(((bf16[512,1024]{1,0:T(8,128)(2,1)}), bf16[128,1024]{1,0:T(8,128)(2,1)}) %reduce-scatter.14.cloned.1.call-update) | async-done | bytes 262160 | tf_op jit(solution)/shard_map/reduce_scatter | solution.py:213
  349.6 26.6 %all-gather.20.cloned.1.call-done = bf16[512,1024]{1,0:T(8,128)(2,1)} async-done(((bf16[128,1024]{1,0:T(8,128)(2,1)}), bf16[512,1024]{1,0:T(8,128)(2,1)}) %all-gather.20.cloned.1.call-update) | async-done | bytes 1048592 | tf_op jit(solution)/shard_map/all_gather | solution.py:228
  379.1 3.8 fusion.2
  391.6 6.1 %convert_bitcast_fusion = bf16[1024,2048]{0,1:T(8,128)(2,1)} fusion(bf16[512,2048]{1,0:T(8,128)(2,1)} %get-tuple-element.99, bf16[512,1024]{1,0:T(8,128)(2,1)S(1)} %copy-done.37), kind=kOutput, calls=%fused_computation.9 | convolution fusion | flops 2149580800 | bytes 7340032 | tf_op jit(solution)/shard_map/dot_general | solution.py:204
  397.7 6.5 %copy.115 = bf16[1024,2048]{1,0:T(8,128)(2,1)} copy(bf16[1024,2048]{0,1:T(8,128)(2,1)} %convert_bitcast_fusion) | data formatting | bytes 8388608
  405.5 9.0 %convolution_convert_fusion = bf16[1024,4096]{1,0:T(8,128)(2,1)} fusion(bf16[512,1024]{1,0:T(8,128)(2,1)S(1)} %copy-done.36, bf16[512,2048]{1,0:T(8,128)(2,1)} %copy-done.40, bf16[512,2048]{1,0:T(8,128)(2,1)} %copy-done.39), kind=kOutput, calls=%fused_computation | convolution fusion | flops 4307550208 | bytes 13631488 | tf_op jit(solution)/shard_map/dot_general | solution.py:207
  416.3 40.0 %psum.7 = f32[2,1024]{1,0:T(2,128)S(1)} all-reduce(f32[2,1024]{1,0:T(2,128)S(1)} %pad_maximum_fusion.14), channel_id=1, replica_groups=mesh['dp'=8,'tensor'=4] {'dp','tensor'}, use_global_device_ids=true, to_apply=%region_13.14 | all-reduce | flops 2048 | bytes 16384 | tf_op jit(solution)/shard_map/psum | solution.py:276
  462.0 47.7 %reduce-scatter.24.cloned.1.call-done = bf16[128,2048]{1,0:T(8,128)(2,1)} async-done(((bf16[1024,2048]{1,0:T(8,128)(2,1)}), bf16[128,2048]{1,0:T(8,128)(2,1)}) %reduce-scatter.24.cloned.1.call-update) | async-done | bytes 524304
  512.3 3.7 multiply_subtract_fusion.1
  516.0 68.6 %reduce-scatter.20.cloned.1.call-done = bf16[128,4096]{1,0:T(8,128)(2,1)} async-done(((bf16[1024,4096]{1,0:T(8,128)(2,1)}), bf16[128,4096]{1,0:T(8,128)(2,1)}) %reduce-scatter.20.cloned.1.call-update) | async-done | bytes 1048592 | tf_op jit(solution)/shard_map/reduce_scatter | solution.py:218
  587.1 4.9 multiply_subtract_fusion
  (181 shorter events, 64.1 us)
Async XLA Ops:
  7.2 43.0 %all-gather.8.cloned.1.call-start = ((), (), s32[]{:S(2)}) async-start(), calls=%async_computation.7 | async-start | bytes 1310720 | tf_op jit(solution)/shard_map/all_gather | solution.py:159
  21.8 56.1 %all-gather.10.cloned.1.call-start = ((), (), s32[]{:S(2)}) async-start(), calls=%async_computation.8 | async-start | bytes 1769472 | tf_op jit(solution)/shard_map/all_gather | solution.py:148
  24.6 89.9 %reduce-scatter.12.cloned.1.call-start = ((), (), s32[]{:S(2)}) async-start(), calls=%async_computation.9 | async-start | bytes 1310720 | tf_op jit(solution)/shard_map/reduce_scatter | solution.py:173
  24.8 58.2 %copy-start.7 = (pred[512,512]{0,1:T(8,128)(4,1)}, pred[512,512]{0,1:T(8,128)(4,1)S(1)}, u32[]{:S(2)}) copy-start(pred[512,512]{0,1:T(8,128)(4,1)S(1)} %iota_compare_fusion) | copy-start | bytes 786436
  87.1 57.1 %all-gather.12.cloned.1.call-start = ((), (), s32[]{:S(2)}) async-start(), calls=%async_computation.10 | async-start | bytes 1310720 | tf_op jit(solution)/shard_map/all_gather | solution.py:178
  117.6 84.2 %all-gather.14.cloned.1.call-start = ((), (), s32[]{:S(2)}) async-start(), calls=%async_computation.11 | async-start | bytes 9437184 | tf_op jit(solution)/shard_map/all_gather | solution.py:160
  120.2 111.6 %all-gather.18.cloned.1.call-start = ((), (), s32[]{:S(2)}) async-start(), calls=%async_computation.14 | async-start | bytes 1310720 | tf_op jit(solution)/shard_map/all_gather | solution.py:162
  122.0 148.9 %all-gather.16.cloned.1.call-start = ((), (), s32[]{:S(2)}) async-start(), calls=%async_computation.12 | async-start | bytes 4718592 | tf_op jit(solution)/shard_map/all_gather | solution.py:161
  124.4 193.9 %reduce-scatter.16.cloned.1.call-start = ((), (), s32[]{:S(2)}) async-start(), calls=%async_computation.15 | async-start | bytes 1310720 | tf_op jit(solution)/shard_map/reduce_scatter | solution.py:201
  290.8 56.2 %reduce-scatter.14.cloned.1.call-start = ((), (), s32[]{:S(2)}) async-start(), calls=%async_computation.13 | async-start | bytes 1310720 | tf_op jit(solution)/shard_map/reduce_scatter | solution.py:213
  297.2 78.9 %all-gather.20.cloned.1.call-start = ((), (), s32[]{:S(2)}) async-start(), calls=%async_computation.16 | async-start | bytes 1310720 | tf_op jit(solution)/shard_map/all_gather | solution.py:228
  349.5 65.2 %reduce-scatter.18.cloned.1.call-start = ((), (), s32[]{:S(2)}) async-start(), calls=%async_computation.17 | async-start | bytes 1310720 | tf_op jit(solution)/shard_map/reduce_scatter | solution.py:256
  387.3 71.6 %reduce-scatter.22.cloned.1.call-start = ((), (), s32[]{:S(2)}) async-start(), calls=%async_computation.19 | async-start | bytes 1769472
  391.5 118.2 %reduce-scatter.24.cloned.1.call-start = ((), (), s32[]{:S(2)}) async-start(), calls=%async_computation.20 | async-start | bytes 4718592
  404.2 180.4 %reduce-scatter.20.cloned.1.call-start = ((), (), s32[]{:S(2)}) async-start(), calls=%async_computation.18 | async-start | bytes 9437184 | tf_op jit(solution)/shard_map/reduce_scatter | solution.py:218
  414.5 42.4 %copy-start.10 = (f32[128,1024]{1,0:T(8,128)S(1)}, f32[128,1024]{1,0:T(8,128)}, u32[]{:S(2)}) copy-start(f32[128,1024]{1,0:T(8,128)} %get-tuple-element.94) | copy-start | bytes 1572868
  414.6 45.6 %copy-start.19 = (f32[2,128,128]{2,1,0:T(8,128)S(1)}, f32[2,128,128]{2,1,0:T(8,128)}, u32[]{:S(2)}) copy-start(f32[2,128,128]{2,1,0:T(8,128)} %param.25) | copy-start | bytes 393220
  414.6 45.6 %copy-start.26 = (f32[2,128,128]{2,1,0:T(8,128)S(1)}, f32[2,128,128]{2,1,0:T(8,128)}, u32[]{:S(2)}) copy-start(f32[2,128,128]{2,1,0:T(8,128)} %param.32) | copy-start | bytes 393220
  414.6 45.6 %copy-start.27 = (f32[2,128,128]{2,1,0:T(8,128)S(1)}, f32[2,128,128]{2,1,0:T(8,128)}, u32[]{:S(2)}) copy-start(f32[2,128,128]{2,1,0:T(8,128)} %param.33) | copy-start | bytes 393220
  414.6 46.4 %copy-start.13 = (f32[4,128,128]{2,1,0:T(8,128)S(1)}, f32[4,128,128]{2,1,0:T(8,128)}, u32[]{:S(2)}) copy-start(f32[4,128,128]{2,1,0:T(8,128)} %param.24) | copy-start | bytes 786436
  414.6 46.4 %copy-start.24 = (f32[4,128,128]{2,1,0:T(8,128)S(1)}, f32[4,128,128]{2,1,0:T(8,128)}, u32[]{:S(2)}) copy-start(f32[4,128,128]{2,1,0:T(8,128)} %param.30) | copy-start | bytes 786436
  414.6 46.4 %copy-start.25 = (f32[4,128,128]{2,1,0:T(8,128)S(1)}, f32[4,128,128]{2,1,0:T(8,128)}, u32[]{:S(2)}) copy-start(f32[4,128,128]{2,1,0:T(8,128)} %param.31) | copy-start | bytes 786436
  460.0 52.3 %copy-start.3 = (f32[16,128,128]{2,1,0:T(8,128)S(1)}, f32[16,128,128]{2,1,0:T(8,128)}, u32[]{:S(2)}) copy-start(f32[16,128,128]{2,1,0:T(8,128)} %param.27) | copy-start | bytes 3145732
  516.0 70.5 %copy-start.2 = (f32[16,2,128,128]{3,2,1,0:T(8,128)S(1)}, f32[16,2,128,128]{3,2,1,0:T(8,128)}, u32[]{:S(2)}) copy-start(f32[16,2,128,128]{3,2,1,0:T(8,128)} %param.26) | copy-start | bytes 6291460
  (33 other events, 305.7 us)
Sparse Core Ops, SparseCore 0:
  21.9 28.2 all-gather.7
  52.6 25.1 all-gather.9
  87.3 27.2 reduce-scatter.11
  117.7 26.4 all-gather.11
  146.5 55.2 all-gather.13
  203.8 27.9 all-gather.17
  234.2 36.7 all-gather.15
  291.0 27.2 reduce-scatter.15
  321.2 25.7 reduce-scatter.13
  349.6 26.4 all-gather.19
  387.4 26.6 reduce-scatter.17
  417.8 37.1 reduce-scatter.21
  458.3 51.3 reduce-scatter.23
  513.1 71.4 reduce-scatter.19
